TPU v7x, 512 devices: a whole 4x8x8 slice. The times are simulated.
512 devices in a mesh: row: 32 (over y, x), col: 16 (over z, core).
Axes of the slice: x: 4, y: 8, z: 8, core: 2. Of those that a mesh axis runs over, the one named last changes fastest.
Arguments:
- gram_panel: float32 [8192, 1024], P('row', 'col'), may hold values from -2973.8 to 2973.8, as said below
- left_factor: bfloat16 [8192, 16384], P('row', 'col'), may hold values from -0.42426407 to 0.42426407
- solved_prev: bfloat16 [16384, 8192], P('row', 'col'), may hold values from -0.59765625 to 0.59765625
- right_block: float32 [1024, 8192], P('row', 'col'), may hold values from -6 to 6
Outputs:
- panel_factor: float32 [8192, 1024], P('row', 'col')
- solved_panel: float32 [1024, 8192], P('row', 'col')
Inputs may be any that keep to these rules, and one draw needn't show every extreme that they name: The rows of gram_panel at the panel's indices minus the product of the corresponding rows of left_factor with their transpose form a symmetric positive definite matrix.
All inputs are finite; a program needn't handle non-finite values.
Results may differ from a plain program's by a relative error of at most 0.0006.
Values may be sent and summed in bfloat16 or wider, within the bound.
No kernel may reach another device: no remote copies, remote signals or barrier semaphores. Data moves between devices by JAX's collectives and lax.ppermute only.
A program may use at most 64 MiB of HBM per device.

v0:
```python
import jax
import jax.numpy as jnp
from jax import lax
from jax.sharding import PartitionSpec as P


def spread(value, axis, source):
    kept = jnp.where(lax.axis_index(axis) == source, value, 0).astype(value.dtype)
    return lax.psum(kept, axis)


def invert(diagonal):
    factor = jnp.linalg.cholesky(diagonal)
    identity = jnp.eye(diagonal.shape[0], dtype=jnp.float32)
    return jax.scipy.linalg.solve_triangular(factor, identity, lower=True)


def body(gram_panel, left_factor, solved_prev, right_block):
    row_count = lax.axis_size("row")
    col_count = lax.axis_size("col")
    row_place = lax.axis_index("row")
    col_place = lax.axis_index("col")
    block_rows = right_block.shape[0]
    col_width = gram_panel.shape[1]
    per_column = row_count // col_count
    strip_width = left_factor.shape[1] // per_column
    chosen = lax.all_gather(left_factor[:block_rows], "row", axis=0, tiled=True)
    portion = chosen
    summed = lax.psum_scatter(
        jnp.einsum("pk,mk->pm", portion, left_factor, preferred_element_type=jnp.float32),
        "col",
        scatter_dimension=0,
        tiled=True,
    )
    update = gram_panel - summed.T
    diag_part = lax.all_gather(update[:block_rows], "row", axis=0, tiled=True)
    diagonal = lax.all_gather(diag_part, "col", axis=1, tiled=True)
    inverse = invert(diagonal)
    inverse_cols = lax.dynamic_slice_in_dim(inverse, col_place * col_width, col_width, 0)
    inverse_part = inverse_cols
    panel_factor = lax.dot_general(
        lax.all_gather(update, "col", axis=1, tiled=True),
        inverse_part,
        (((1,), (1,)), ((), ())),
        precision=lax.Precision.HIGHEST,
    )
    strip_piece = lax.dynamic_slice_in_dim(
        chosen, row_place % per_column * strip_width, strip_width, 1
    )
    strip_piece = spread(strip_piece, "col", row_place // per_column)
    portion = strip_piece
    reduced = right_block - lax.psum_scatter(
        jnp.dot(portion, solved_prev, preferred_element_type=jnp.float32),
        "row",
        scatter_dimension=0,
        tiled=True,
    )
    inverse_rows = lax.dynamic_slice_in_dim(inverse, row_place * block_rows, block_rows, 0)
    inverse_part = inverse_rows
    solved_panel = jnp.dot(
        inverse_part,
        lax.all_gather(reduced, "row", axis=0, tiled=True),
        precision=lax.Precision.HIGHEST,
    )
    return (panel_factor, solved_panel)


def solution(mesh):
    in_specs = (P("row", "col"), P("row", "col"), P("row", "col"), P("row", "col"))
    out_specs = (P("row", "col"), P("row", "col"))
    return jax.shard_map(body, mesh=mesh, in_specs=in_specs, out_specs=out_specs, check_vma=False)
```

profile of v0, /device:TPU:1, one launch (start us, length us, event | category | flops | bytes accessed | tf_op | source)
XLA Modules:
  0.0 915.5 jit_solution(4656776217967420164)
XLA Ops:
  8.8 87.9 %all-gather.5.cloned.1.call-done = bf16[1024,1024]{1,0:T(8,128)(2,1)} async-done(((bf16[32,1024]{1,0:T(8,128)(2,1)}), bf16[1024,1024]{1,0:T(8,128)(2,1)}) %all-gather.5.cloned.1.call-update) | async-done | bytes 2097168 | tf_op jit(solution)/shard_map/all_gather | solution.py:27
  99.2 3.4 fusion.77
  102.7 115.2 %all-reduce.3.cloned.1.call-done = bf16[1024,512]{1,0:T(8,128)(2,1)} async-done(((bf16[1024,512]{1,0:T(8,128)(2,1)}), bf16[1024,512]{1,0:T(8,128)(2,1)}) %all-reduce.3.cloned.1.call-update) | async-done | bytes 1048592 | tf_op jit(solution)/shard_map/psum | solution.py:9
  218.0 3.3 fusion.78
  221.3 57.3 %reduce-scatter.3.cloned.1.call-done = f32[64,256]{1,0:T(8,128)} async-done(((f32[1024,256]{1,0:T(8,128)}), f32[64,256]{1,0:T(8,128)}) %reduce-scatter.3.cloned.1.call-update) | async-done | bytes 65552 | tf_op jit(solution)/shard_map/reduce_scatter | solution.py:29
  279.6 38.7 %all_gather.17 = f32[1024,64]{1,0:T(8,128)S(1)} all-gather(f32[32,64]{1,0:T(8,128)S(1)} %copy.7), channel_id=1, replica_groups=mesh['row'=32,'col'=16] {'row'}, dimensions={0}, use_global_device_ids=true | all-gather | bytes 270336 | tf_op jit(solution)/shard_map/all_gather | solution.py:36
  319.3 180.5 %reduce-scatter.5.cloned.1.call-done = f32[32,512]{1,0:T(8,128)} async-done(((f32[1024,512]{1,0:T(8,128)}), f32[32,512]{1,0:T(8,128)}) %reduce-scatter.5.cloned.1.call-update) | async-done | bytes 65552 | tf_op jit(solution)/shard_map/reduce_scatter | solution.py:52
  504.2 47.7 %all-gather.9.cloned.1.call-done = f32[1024,1024]{0,1:T(8,128)} async-done(((f32[1024,64]{0,1:T(8,128)}), f32[1024,1024]{0,1:T(8,128)}) %all-gather.9.cloned.1.call-update) | async-done | bytes 4194320 | tf_op jit(solution)/shard_map/all_gather | solution.py:37
  551.8 5.8 copy.9
  557.7 4.4 fusion
  564.1 11.7 %cholesky.223 = f32[128,128]{1,0:T(8,128)S(1)} custom-call(f32[128,128]{1,0:T(8,128)S(1)} %cholesky.580), custom_call_target="Cholesky" | custom-call | tf_op jit(solution)/shard_map/jit(cholesky)/cholesky | solution.py:13
  575.9 9.8 %custom-call.63 = f32[1,128,128]{1,2,0:T(8,128)S(1)} custom-call(f32[1,128,128]{2,1,0:T(8,128)S(1)} %get-tuple-element.66), custom_call_target="InvertDiagBlocksLowerTriangular" | custom-call | tf_op jit(solution)/shard_map/jit(cholesky)/cholesky | solution.py:13
  592.1 11.9 %cholesky.244 = f32[128,128]{1,0:T(8,128)S(1)} custom-call(f32[128,128]{1,0:T(8,128)S(1)} %cholesky.584), custom_call_target="Cholesky" | custom-call | tf_op jit(solution)/shard_map/jit(cholesky)/cholesky | solution.py:13
  604.6 9.8 %custom-call.64 = f32[1,128,128]{1,2,0:T(8,128)S(1)} custom-call(f32[1,128,128]{2,1,0:T(8,128)S(1)} %get-tuple-element.63), custom_call_target="InvertDiagBlocksLowerTriangular" | custom-call | tf_op jit(solution)/shard_map/jit(cholesky)/cholesky | solution.py:13
  617.8 11.7 %cholesky.468 = f32[128,128]{1,0:T(8,128)S(1)} custom-call(f32[128,128]{1,0:T(8,128)S(1)} %cholesky.589), custom_call_target="Cholesky" | custom-call | tf_op jit(solution)/shard_map/jit(cholesky)/cholesky | solution.py:13
  630.8 9.8 %custom-call.65 = f32[1,128,128]{1,2,0:T(8,128)S(1)} custom-call(f32[1,128,128]{2,1,0:T(8,128)S(1)} %get-tuple-element.60), custom_call_target="InvertDiagBlocksLowerTriangular" | custom-call | tf_op jit(solution)/shard_map/jit(cholesky)/cholesky | solution.py:13
  644.2 11.9 %cholesky.487 = f32[128,128]{1,0:T(8,128)S(1)} custom-call(f32[128,128]{1,0:T(8,128)S(1)} %cholesky.594), custom_call_target="Cholesky" | custom-call | tf_op jit(solution)/shard_map/jit(cholesky)/cholesky | solution.py:13
  657.3 9.8 %custom-call.66 = f32[1,128,128]{1,2,0:T(8,128)S(1)} custom-call(f32[1,128,128]{2,1,0:T(8,128)S(1)} %get-tuple-element.57), custom_call_target="InvertDiagBlocksLowerTriangular" | custom-call | tf_op jit(solution)/shard_map/jit(cholesky)/cholesky | solution.py:13
  670.6 11.7 %cholesky.506 = f32[128,128]{1,0:T(8,128)S(1)} custom-call(f32[128,128]{1,0:T(8,128)S(1)} %cholesky.599), custom_call_target="Cholesky" | custom-call | tf_op jit(solution)/shard_map/jit(cholesky)/cholesky | solution.py:13
  683.6 10.2 %custom-call.67 = f32[1,128,128]{1,2,0:T(8,128)S(1)} custom-call(f32[1,128,128]{2,1,0:T(8,128)S(1)} %get-tuple-element.54), custom_call_target="InvertDiagBlocksLowerTriangular" | custom-call | tf_op jit(solution)/shard_map/jit(cholesky)/cholesky | solution.py:13
  697.1 11.7 %cholesky.526 = f32[128,128]{1,0:T(8,128)S(1)} custom-call(f32[128,128]{1,0:T(8,128)S(1)} %cholesky.604), custom_call_target="Cholesky" | custom-call | tf_op jit(solution)/shard_map/jit(cholesky)/cholesky | solution.py:13
  710.2 9.8 %custom-call.68 = f32[1,128,128]{1,2,0:T(8,128)S(1)} custom-call(f32[1,128,128]{2,1,0:T(8,128)S(1)} %get-tuple-element.51), custom_call_target="InvertDiagBlocksLowerTriangular" | custom-call | tf_op jit(solution)/shard_map/jit(cholesky)/cholesky | solution.py:13
  723.0 11.9 %cholesky.546 = f32[128,128]{1,0:T(8,128)S(1)} custom-call(f32[128,128]{1,0:T(8,128)S(1)} %cholesky.609), custom_call_target="Cholesky" | custom-call | tf_op jit(solution)/shard_map/jit(cholesky)/cholesky | solution.py:13
  736.2 9.8 %custom-call.69 = f32[1,128,128]{1,2,0:T(8,128)S(1)} custom-call(f32[1,128,128]{2,1,0:T(8,128)S(1)} %get-tuple-element.48), custom_call_target="InvertDiagBlocksLowerTriangular" | custom-call | tf_op jit(solution)/shard_map/jit(cholesky)/cholesky | solution.py:13
  748.7 11.7 %cholesky.564 = f32[128,128]{1,0:T(8,128)S(1)} custom-call(f32[128,128]{1,0:T(8,128)S(1)} %convolution_subtract_fusion.11), custom_call_target="Cholesky" | custom-call | tf_op jit(solution)/shard_map/jit(cholesky)/cholesky | solution.py:13
  767.4 4.8 select_select_fusion
  772.3 22.5 %while.1 = (s32[]{:T(128)}, f32[1024,1024]{1,0:T(8,128)}, s32[8,2]{0,1:T(2,128)S(1)}, f32[8,128,128]{2,1,0:T(8,128)S(1)}, s32[]{:T(128)}) while((s32[]{:T(128)}, f32[1024,1024]{1,0:T(8,128)}, s32[8,2]{0,1:T(2,128)S(1)}, f32[8,128,128]{2,1,0:T(8,128)S(1)}, s32[]{:T(128)}) %tuple.61), condition=%wide.while_cond, body=%wide.while_body.sunk | while | flops 2 | bytes 131181 | solution.py:15
  794.7 78.8 %custom-call.70 = f32[8,128,128]{1,2,0:T(8,128)S(1)} custom-call(f32[8,128,128]{2,1,0:T(8,128)S(1)} %get-tuple-element.9), custom_call_target="InvertDiagBlocksLowerTriangular" | custom-call | tf_op jit(solution)/shard_map/jit(_solve_triangular)/triangular_solve | solution.py:15
  888.8 2.6 convolution_subtract_fusion.2
  892.9 2.8 convolution_subtract_fusion.1
  897.2 3.5 convolution_subtract_fusion.3
  902.2 3.6 fusion.53
  (114 shorter events, 91.8 us)
Async XLA Ops:
  7.2 210.8 %copy-start = (bf16[512,512]{1,0:T(8,128)(2,1)S(1)}, bf16[512,512]{1,0:T(8,128)(2,1)}, u32[]{:S(2)}) copy-start(bf16[512,512]{1,0:T(8,128)(2,1)} %param.6) | copy-start | bytes 1572868
  7.2 89.6 %all-gather.5.cloned.1.call-start = ((), (), s32[]{:S(2)}) async-start(), calls=%async_computation.2 | async-start | bytes 2162688 | tf_op jit(solution)/shard_map/all_gather | solution.py:27
  8.8 209.2 %all-reduce.3.cloned.1.call-start = ((), (), s32[]{:S(2)}) async-start(), calls=%async_computation.6 | async-start | bytes 2097152 | tf_op jit(solution)/shard_map/psum | solution.py:9
  99.2 179.5 %reduce-scatter.3.cloned.1.call-start = ((), (), s32[]{:S(2)}) async-start(), calls=%async_computation.3 | async-start | bytes 1114112 | tf_op jit(solution)/shard_map/reduce_scatter | solution.py:29
  102.6 176.0 %copy-start.4 = (f32[256,64]{0,1:T(8,128)S(1)}, f32[256,64]{0,1:T(8,128)}, u32[]{:S(2)}) copy-start(f32[256,64]{0,1:T(8,128)} %param.4) | copy-start | bytes 196612
  102.7 397.2 %copy-start.5 = (f32[32,512]{1,0:T(8,128)S(1)}, f32[32,512]{1,0:T(8,128)}, u32[]{:S(2)}) copy-start(f32[32,512]{1,0:T(8,128)} %param.7) | copy-start | bytes 196612
  102.7 397.1 %reduce-scatter.5.cloned.1.call-start = ((), (), s32[]{:S(2)}) async-start(), calls=%async_computation.7 | async-start | bytes 2162688 | tf_op jit(solution)/shard_map/reduce_scatter | solution.py:52
  221.3 330.6 %all-gather.9.cloned.1.call-start = ((), (), s32[]{:S(2)}) async-start(), calls=%async_computation.5 | async-start | bytes 4456448 | tf_op jit(solution)/shard_map/all_gather | solution.py:37
  279.5 224.6 %copy-start.3 = (f32[256,64]{0,1:T(8,128)}, f32[256,64]{0,1:T(8,128)S(1)}, u32[]{:S(2)}) copy-start(f32[256,64]{0,1:T(8,128)S(1)} %bitcast_subtract_fusion) | copy-start | bytes 196612
  319.2 582.9 %all-gather.11.cloned.1.call-start = ((), (), s32[]{:S(2)}) async-start(), calls=%async_computation.8 | async-start | bytes 2162688 | tf_op jit(solution)/shard_map/all_gather | solution.py:62
  501.3 404.4 %all-gather.7.cloned.1.call-start = ((), (), s32[]{:S(2)}) async-start(), calls=%async_computation.4 | async-start | bytes 1114112 | tf_op jit(solution)/shard_map/all_gather | solution.py:42
  562.1 2.0 copy-start.2
  873.6 4.7 copy-start.1
Sparse Core Ops, SparseCore 0:
  11.8 84.9 all-gather.4
  99.3 118.6 all-reduce.2
  221.0 57.5 reduce-scatter.2
  282.9 216.8 reduce-scatter.4
  502.0 49.8 all-gather.8
  555.9 77.5 all-gather.10
  636.4 43.9 all-gather.6
where the time goes:
time: 920 us; the launch traced here: 915 us
  waiting for transfers between devices  489 us (53%)
  other arithmetic  268 us (29%)
  matrix products  64.5 us (7%)
  blocking collectives  38.7 us (4%)
  local copies, waits for them, and re-layouts  35.2 us (4%)
  between operations  19.8 us (2%)
    reduce_scatter x1, waiting for transfers between devices, body(): lax.psum_scatter(jnp.dot(portion, solved_prev, preferred_element_type=jnp...  181 us
    another operation x30, other arithmetic, invert(): factor = jnp.linalg.cholesky(diagonal)  172 us
    psum x1, waiting for transfers between devices, spread(): return lax.psum(kept, axis)  115 us
    all_gather x1, waiting for transfers between devices, body(): chosen = lax.all_gather(left_factor[:block_rows], 'row', axis=0, tiled=True)  87.9 us
    another operation x3, other arithmetic, invert(): return jax.scipy.linalg.solve_triangular(factor, identity, lower=True)  83.6 us
    reduce_scatter x1, waiting for transfers between devices, body(): lax.psum_scatter(jnp.einsum('pk,mk->pm', portion, left_factor, preferred_...  57.3 us
    all_gather x1, waiting for transfers between devices, body(): diagonal = lax.all_gather(diag_part, 'col', axis=1, tiled=True)  47.7 us
    all_gather x1, blocking collectives, body(): diag_part = lax.all_gather(update[:block_rows], 'row', axis=0, tiled=True)  38.7 us
  transfers between devices with their start and end apart: 7, of which 5 were waited for; matrix products, arithmetic and copies ran while one was open for 39% of the time, Pallas kernels for 0%

commit v1 on v0

--- a/solution.py
+++ b/solution.py
@@ -6,7 +6,7 @@
 
 def spread(value, axis, source):
     kept = jnp.where(lax.axis_index(axis) == source, value, 0).astype(value.dtype)
-    return lax.psum(kept, axis)
+    return jnp.sum(lax.all_gather(kept, axis_name=axis), axis=0)
 
 
 def invert(diagonal):

time: 920 us -> 729 us (0.79)
  waiting for transfers between devices: 489 us -> 280 us
    reduce_scatter x1, waiting for transfers between devices: 181 us -> 0.01 us  [body(): lax.psum_scatter(jnp.dot(portion, solved_prev, preferred_element_type=jnp...]
    psum x1 -> x0, waiting for transfers between devices: 115 us -> none  [spread(): return lax.psum(kept, axis)]
    all_gather x0 -> x1, waiting for transfers between devices: none -> 59.7 us  [spread(): return jnp.sum(lax.all_gather(kept, axis_name=axis), axis=0)]
    all_gather x1, waiting for transfers between devices: 0.01 us -> 43.6 us  [body(): lax.all_gather(reduced, 'row', axis=0, tiled=True)]
    all_gather x1, waiting for transfers between devices: 47.7 us -> 31 us  [body(): diagonal = lax.all_gather(diag_part, 'col', axis=1, tiled=True)]
  transfers between devices with their start and end apart: 7 -> 7, of which waited for: 5 -> 5; matrix products, arithmetic and copies ran while one was open for 39% -> 51% of each run, Pallas kernels for 0% -> 0%
where the time goes in v1:
time: 729 us; the launch traced here: 722 us
  waiting for transfers between devices  280 us (38%)
  other arithmetic  277 us (38%)
  matrix products  68.5 us (9%)
  blocking collectives  40.7 us (6%)
  local copies, waits for them, and re-layouts  35.1 us (5%)
  between operations  19.7 us (3%)
    another operation x30, other arithmetic, invert(): factor = jnp.linalg.cholesky(diagonal)  172 us
    all_gather x1, waiting for transfers between devices, body(): chosen = lax.all_gather(left_factor[:block_rows], 'row', axis=0, tiled=True)  88 us
    another operation x3, other arithmetic, invert(): return jax.scipy.linalg.solve_triangular(factor, identity, lower=True)  84.3 us
    all_gather x1, waiting for transfers between devices, spread(): return jnp.sum(lax.all_gather(kept, axis_name=axis), axis=0)  59.7 us
    reduce_scatter x1, waiting for transfers between devices, body(): lax.psum_scatter(jnp.einsum('pk,mk->pm', portion, left_factor, preferred_...  57.8 us
    all_gather x1, waiting for transfers between devices, body(): lax.all_gather(reduced, 'row', axis=0, tiled=True)  43.6 us
    all_gather x1, blocking collectives, body(): diag_part = lax.all_gather(update[:block_rows], 'row', axis=0, tiled=True)  40.7 us
    another operation x15, matrix products, invert(): return jax.scipy.linalg.solve_triangular(factor, identity, lower=True)  33.6 us
  transfers between devices with their start and end apart: 7, of which 5 were waited for; matrix products, arithmetic and copies ran while one was open for 51% of the time, Pallas kernels for 0%

profile of v1, /device:TPU:1, one launch (start us, length us, event | category | flops | bytes accessed | tf_op | source)
XLA Modules:
  0.0 721.8 jit_solution(335722015555205800)
XLA Ops:
  8.8 88.0 %all-gather.7.cloned.1.call-done = bf16[1024,1024]{1,0:T(8,128)(2,1)} async-done(((bf16[32,1024]{1,0:T(8,128)(2,1)}), bf16[1024,1024]{1,0:T(8,128)(2,1)}) %all-gather.7.cloned.1.call-update) | async-done | bytes 2097168 | tf_op jit(solution)/shard_map/all_gather | solution.py:27
  96.8 3.6 fusion.77
  101.8 57.8 %reduce-scatter.3.cloned.1.call-done = f32[64,256]{1,0:T(8,128)} async-done(((f32[1024,256]{1,0:T(8,128)}), f32[64,256]{1,0:T(8,128)}) %reduce-scatter.3.cloned.1.call-update) | async-done | bytes 65552 | tf_op jit(solution)/shard_map/reduce_scatter | solution.py:29
  160.5 40.7 %all_gather.23 = f32[1024,64]{1,0:T(8,128)S(1)} all-gather(f32[32,64]{1,0:T(8,128)S(1)} %copy.7), channel_id=1, replica_groups=mesh['row'=32,'col'=16] {'row'}, dimensions={0}, use_global_device_ids=true | all-gather | bytes 270336 | tf_op jit(solution)/shard_map/all_gather | solution.py:36
  202.2 59.7 %all-gather.15.cloned.1.call-done = bf16[16384,512]{1,0:T(8,128)(2,1)} async-done(((bf16[1024,512]{1,0:T(8,128)(2,1)}), bf16[16384,512]{1,0:T(8,128)(2,1)}) %all-gather.15.cloned.1.call-update) | async-done | bytes 16777232 | tf_op jit(solution)/shard_map/all_gather | solution.py:9
  261.9 8.9 %reduce_sum.12 = bf16[1024,512]{1,0:T(8,128)(2,1)S(1)} reduce(bf16[16,1024,512]{2,1,0:T(8,128)(2,1)} %bitcast.110, bf16[]{:T(256)} %constant.321.clone.1), dimensions={0}, to_apply=%region_17.18 | reduce | flops 7864320 | bytes 17825794 | tf_op jit(solution)/shard_map/reduce_sum | solution.py:9
  276.8 31.0 %all-gather.11.cloned.1.call-done = f32[1024,1024]{0,1:T(8,128)} async-done(((f32[1024,64]{0,1:T(8,128)}), f32[1024,1024]{0,1:T(8,128)}) %all-gather.11.cloned.1.call-update) | async-done | bytes 4194320 | tf_op jit(solution)/shard_map/all_gather | solution.py:37
  307.7 5.8 copy.9
  313.6 4.4 fusion
  320.0 11.7 %cholesky.223 = f32[128,128]{1,0:T(8,128)S(1)} custom-call(f32[128,128]{1,0:T(8,128)S(1)} %cholesky.580), custom_call_target="Cholesky" | custom-call | tf_op jit(solution)/shard_map/jit(cholesky)/cholesky | solution.py:13
  331.8 9.8 %custom-call.63 = f32[1,128,128]{1,2,0:T(8,128)S(1)} custom-call(f32[1,128,128]{2,1,0:T(8,128)S(1)} %get-tuple-element.66), custom_call_target="InvertDiagBlocksLowerTriangular" | custom-call | tf_op jit(solution)/shard_map/jit(cholesky)/cholesky | solution.py:13
  348.0 11.9 %cholesky.244 = f32[128,128]{1,0:T(8,128)S(1)} custom-call(f32[128,128]{1,0:T(8,128)S(1)} %cholesky.584), custom_call_target="Cholesky" | custom-call | tf_op jit(solution)/shard_map/jit(cholesky)/cholesky | solution.py:13
  360.5 9.8 %custom-call.64 = f32[1,128,128]{1,2,0:T(8,128)S(1)} custom-call(f32[1,128,128]{2,1,0:T(8,128)S(1)} %get-tuple-element.63), custom_call_target="InvertDiagBlocksLowerTriangular" | custom-call | tf_op jit(solution)/shard_map/jit(cholesky)/cholesky | solution.py:13
  373.7 11.7 %cholesky.468 = f32[128,128]{1,0:T(8,128)S(1)} custom-call(f32[128,128]{1,0:T(8,128)S(1)} %cholesky.589), custom_call_target="Cholesky" | custom-call | tf_op jit(solution)/shard_map/jit(cholesky)/cholesky | solution.py:13
  386.7 9.8 %custom-call.65 = f32[1,128,128]{1,2,0:T(8,128)S(1)} custom-call(f32[1,128,128]{2,1,0:T(8,128)S(1)} %get-tuple-element.60), custom_call_target="InvertDiagBlocksLowerTriangular" | custom-call | tf_op jit(solution)/shard_map/jit(cholesky)/cholesky | solution.py:13
  400.0 11.9 %cholesky.487 = f32[128,128]{1,0:T(8,128)S(1)} custom-call(f32[128,128]{1,0:T(8,128)S(1)} %cholesky.594), custom_call_target="Cholesky" | custom-call | tf_op jit(solution)/shard_map/jit(cholesky)/cholesky | solution.py:13
  413.2 9.8 %custom-call.66 = f32[1,128,128]{1,2,0:T(8,128)S(1)} custom-call(f32[1,128,128]{2,1,0:T(8,128)S(1)} %get-tuple-element.57), custom_call_target="InvertDiagBlocksLowerTriangular" | custom-call | tf_op jit(solution)/shard_map/jit(cholesky)/cholesky | solution.py:13
  426.5 11.7 %cholesky.506 = f32[128,128]{1,0:T(8,128)S(1)} custom-call(f32[128,128]{1,0:T(8,128)S(1)} %cholesky.599), custom_call_target="Cholesky" | custom-call | tf_op jit(solution)/shard_map/jit(cholesky)/cholesky | solution.py:13
  439.6 10.2 %custom-call.67 = f32[1,128,128]{1,2,0:T(8,128)S(1)} custom-call(f32[1,128,128]{2,1,0:T(8,128)S(1)} %get-tuple-element.54), custom_call_target="InvertDiagBlocksLowerTriangular" | custom-call | tf_op jit(solution)/shard_map/jit(cholesky)/cholesky | solution.py:13
  453.0 11.7 %cholesky.526 = f32[128,128]{1,0:T(8,128)S(1)} custom-call(f32[128,128]{1,0:T(8,128)S(1)} %cholesky.604), custom_call_target="Cholesky" | custom-call | tf_op jit(solution)/shard_map/jit(cholesky)/cholesky | solution.py:13
  466.0 9.8 %custom-call.68 = f32[1,128,128]{1,2,0:T(8,128)S(1)} custom-call(f32[1,128,128]{2,1,0:T(8,128)S(1)} %get-tuple-element.51), custom_call_target="InvertDiagBlocksLowerTriangular" | custom-call | tf_op jit(solution)/shard_map/jit(cholesky)/cholesky | solution.py:13
  478.9 11.9 %cholesky.546 = f32[128,128]{1,0:T(8,128)S(1)} custom-call(f32[128,128]{1,0:T(8,128)S(1)} %cholesky.609), custom_call_target="Cholesky" | custom-call | tf_op jit(solution)/shard_map/jit(cholesky)/cholesky | solution.py:13
  492.0 9.8 %custom-call.69 = f32[1,128,128]{1,2,0:T(8,128)S(1)} custom-call(f32[1,128,128]{2,1,0:T(8,128)S(1)} %get-tuple-element.48), custom_call_target="InvertDiagBlocksLowerTriangular" | custom-call | tf_op jit(solution)/shard_map/jit(cholesky)/cholesky | solution.py:13
  504.5 11.7 %cholesky.564 = f32[128,128]{1,0:T(8,128)S(1)} custom-call(f32[128,128]{1,0:T(8,128)S(1)} %convolution_subtract_fusion.11), custom_call_target="Cholesky" | custom-call | tf_op jit(solution)/shard_map/jit(cholesky)/cholesky | solution.py:13
  523.1 4.9 select_select_fusion
  528.0 22.4 %while.1 = (s32[]{:T(128)}, f32[1024,1024]{1,0:T(8,128)}, s32[8,2]{0,1:T(2,128)S(1)}, f32[8,128,128]{2,1,0:T(8,128)S(1)}, s32[]{:T(128)}) while((s32[]{:T(128)}, f32[1024,1024]{1,0:T(8,128)}, s32[8,2]{0,1:T(2,128)S(1)}, f32[8,128,128]{2,1,0:T(8,128)S(1)}, s32[]{:T(128)}) %tuple.61), condition=%wide.while_cond, body=%wide.while_body.sunk | while | flops 2 | bytes 131181 | solution.py:15
  550.3 79.4 %custom-call.70 = f32[8,128,128]{1,2,0:T(8,128)} custom-call(f32[8,128,128]{2,1,0:T(8,128)S(1)} %get-tuple-element.9), custom_call_target="InvertDiagBlocksLowerTriangular" | custom-call | tf_op jit(solution)/shard_map/jit(_solve_triangular)/triangular_solve | solution.py:15
  635.6 2.8 constant_dynamic-update-slice_fusion.16
  654.5 4.0 convolution_subtract_fusion.1
  659.9 3.6 convolution_subtract_fusion.3
  667.6 43.6 %all-gather.13.cloned.1.call-done = f32[1024,512]{1,0:T(8,128)} async-done(((f32[32,512]{1,0:T(8,128)}), f32[1024,512]{1,0:T(8,128)}) %all-gather.13.cloned.1.call-update) | async-done | bytes 2097168 | tf_op jit(solution)/shard_map/all_gather | solution.py:62
  711.1 3.6 fusion.53
  (123 shorter events, 97.2 us)
Async XLA Ops:
  7.2 263.7 %copy-start = (bf16[512,512]{1,0:T(8,128)(2,1)S(1)}, bf16[512,512]{1,0:T(8,128)(2,1)}, u32[]{:S(2)}) copy-start(bf16[512,512]{1,0:T(8,128)(2,1)} %param.6) | copy-start | bytes 1572868
  7.2 89.6 %all-gather.7.cloned.1.call-start = ((), (), s32[]{:S(2)}) async-start(), calls=%async_computation.2 | async-start | bytes 2162688 | tf_op jit(solution)/shard_map/all_gather | solution.py:27
  8.8 150.8 %copy-start.8 = (f32[256,64]{0,1:T(8,128)S(1)}, f32[256,64]{0,1:T(8,128)}, u32[]{:S(2)}) copy-start(f32[256,64]{0,1:T(8,128)} %param.4) | copy-start | bytes 196612
  8.8 150.8 %reduce-scatter.3.cloned.1.call-start = ((), (), s32[]{:S(2)}) async-start(), calls=%async_computation.3 | async-start | bytes 1114112 | tf_op jit(solution)/shard_map/reduce_scatter | solution.py:29
  96.8 3.7 copy-start.5
  100.4 161.5 %all-gather.15.cloned.1.call-start = ((), (), s32[]{:S(2)}) async-start(), calls=%async_computation.8 | async-start | bytes 17825792 | tf_op jit(solution)/shard_map/all_gather | solution.py:9
  101.7 206.0 %all-gather.11.cloned.1.call-start = ((), (), s32[]{:S(2)}) async-start(), calls=%async_computation.5 | async-start | bytes 4456448 | tf_op jit(solution)/shard_map/all_gather | solution.py:37
  160.4 110.4 %copy-start.7 = (f32[256,64]{0,1:T(8,128)}, f32[256,64]{0,1:T(8,128)S(1)}, u32[]{:S(2)}) copy-start(f32[256,64]{0,1:T(8,128)S(1)} %bitcast_subtract_fusion) | copy-start | bytes 196612
  202.1 430.2 %reduce-scatter.5.cloned.1.call-start = ((), (), s32[]{:S(2)}) async-start(), calls=%async_computation.6 | async-start | bytes 2162688 | tf_op jit(solution)/shard_map/reduce_scatter | solution.py:52
  272.9 392.0 %all-gather.9.cloned.1.call-start = ((), (), s32[]{:S(2)}) async-start(), calls=%async_computation.4 | async-start | bytes 1114112 | tf_op jit(solution)/shard_map/all_gather | solution.py:42
  276.7 434.4 %all-gather.13.cloned.1.call-start = ((), (), s32[]{:S(2)}) async-start(), calls=%async_computation.7 | async-start | bytes 2162688 | tf_op jit(solution)/shard_map/all_gather | solution.py:62
  318.0 2.0 copy-start.3
  523.0 109.3 %copy-start.9 = (f32[32,512]{1,0:T(8,128)S(1)}, f32[32,512]{1,0:T(8,128)}, u32[]{:S(2)}) copy-start(f32[32,512]{1,0:T(8,128)} %param.7) | copy-start | bytes 196612
  633.8 4.6 copy-start.2
  633.8 6.2 copy-start.6
  654.5 4.0 copy-start.4
  659.9 54.8 %copy-start.1 = (bf16[512,512]{1,0:T(8,128)(2,1)S(1)}, bf16[512,512]{1,0:T(8,128)(2,1)}, u32[]{:S(2)}) copy-start(bf16[512,512]{1,0:T(8,128)(2,1)} %param.6) | copy-start | bytes 1572868
Sparse Core Ops, SparseCore 0:
  11.8 84.9 all-gather.6
  100.5 59.0 reduce-scatter.2
  161.9 99.9 all-gather.14
  264.1 43.5 all-gather.10
  312.6 215.5 reduce-scatter.4
  530.8 45.9 all-gather.8
  633.9 77.1 all-gather.12
